TPU v7x, 32 devices: a whole 2x2x4 slice. The times are simulated.
32 devices in a mesh: rows: 2 (over x), cols: 16 (over z, y, core).
Axes of the slice: x: 2, y: 2, z: 4, core: 2. Of those that a mesh axis runs over, the one named last changes fastest.
Arguments:
- queries: bfloat16 [8192, 1024], P(('rows', 'cols')), may hold values from -1 to 1
- attn_out: bfloat16 [8192, 1024], P(('rows', 'cols')), may hold values from -6 to 6
- out_grad: bfloat16 [8192, 1024], P(('rows', 'cols')), may hold values from -96 to 96
- log_norm: float32 [8192, 8], P(('rows', 'cols')), may hold values from 7.5 to 8.5
- leaf_kv: bfloat16 [8192, 256], P(('rows', 'cols')), may hold values from -1 to 1
- root_kv: bfloat16 [2048, 256], P('cols'), may hold values from -1 to 1
- branch_kv: bfloat16 [4, 1024, 256], P('rows', 'cols'), may hold values from -1 to 1
- branch_len: int32 [4], replicated, may hold values from 256 to 1024, as said below
- segment_ids: int32 [32, 256], P(('rows', 'cols')), may hold values from 0 to 7, never falling along the last dimension, each value on 1 to 128 neighbouring positions
- segment_branch: int32 [32, 8], P(('rows', 'cols')), may hold values from 0 to 1
Outputs:
- query_grad: bfloat16 [8192, 1024], P(('rows', 'cols'))
- leaf_kv_grad: float32 [8192, 256], P(('rows', 'cols'))
- root_kv_grad: float32 [2048, 256], P('cols')
- branch_kv_grad: float32 [4, 1024, 256], P('rows', 'cols')
Inputs may be any that keep to these rules, and one draw needn't show every extreme that they name: `branch_len`: every branch has between 256 and 1024 live slots; some branch has exactly 1024 and some exactly 256. `segment_ids`: never falling along a device's tokens; each segment has 1 to 128 tokens, one exactly 128. `segment_branch`: a segment on row r extends branch r * 2 + value.
All inputs are finite; a program needn't handle non-finite values.
Results may differ from a plain program's by a relative error of at most 0.0041.
Values may be sent and summed in bfloat16 or wider, within the bound.
A program may use at most 64 MiB of HBM per device.

v0:
```python
from functools import partial
import jax
import jax.numpy as jnp
from jax import lax
from jax.sharding import PartitionSpec as P

HEADS = 8
HD = 128
BR_DEV = 2
SEGS = 8


def block_grads(query_heads, grad_heads, log_norm, row_delta, key_rows, allowed):
    scale = HD ** (-0.5)
    keys_part = key_rows[:, :HD]
    values_part = key_rows[:, HD:]
    scores = (
        jnp.einsum("thd,kd->thk", query_heads, keys_part, preferred_element_type=jnp.float32)
        * scale
    )
    weights = jnp.where(allowed[:, None, :], jnp.exp(scores - log_norm[:, :, None]), 0.0)
    dweight = jnp.einsum("thd,kd->thk", grad_heads, values_part, preferred_element_type=jnp.float32)
    dscore = weights * (dweight - row_delta[:, :, None])
    weight_b = weights.astype(jnp.bfloat16)
    dscore_b = dscore.astype(jnp.bfloat16)
    query_part = (
        jnp.einsum("thk,kd->thd", dscore_b, keys_part, preferred_element_type=jnp.float32) * scale
    )
    key_grad = (
        jnp.einsum("thk,thd->kd", dscore_b, query_heads, preferred_element_type=jnp.float32) * scale
    )
    value_grad = jnp.einsum("thk,thd->kd", weight_b, grad_heads, preferred_element_type=jnp.float32)
    return (query_part, jnp.concatenate([key_grad, value_grad], axis=1))


def sweep_keys(query_heads, grad_heads, log_norm, row_delta, key_rows, allowed_of):
    count_rows = key_rows.shape[0]
    block_rows = 512 if count_rows % 512 == 0 else count_rows

    def visit_block(query_sum, block_index):
        offset = block_index * block_rows
        key_block = lax.dynamic_slice_in_dim(key_rows, offset, block_rows, 0)
        query_part, key_grads = block_grads(
            query_heads, grad_heads, log_norm, row_delta, key_block, allowed_of(offset, block_rows)
        )
        return (query_sum + query_part, key_grads)

    start_sum = jnp.zeros(query_heads.shape, jnp.float32)
    query_sum, key_grads = lax.scan(
        visit_block, start_sum, jnp.arange(count_rows // block_rows, dtype=jnp.int32)
    )
    return (query_sum, key_grads.reshape(count_rows, key_rows.shape[1]))


def shards(
    queries,
    attn_out,
    out_grad,
    log_norm,
    leaf_kv,
    root_kv,
    branch_kv,
    branch_len,
    segment_ids,
    segment_branch,
):
    tokens = queries.shape[0]
    query_heads = queries.reshape(tokens, HEADS, HD)
    grad_heads = out_grad.reshape(tokens, HEADS, HD)
    out_heads = attn_out.reshape(tokens, HEADS, HD)
    row_delta = jnp.sum(grad_heads.astype(jnp.float32) * out_heads.astype(jnp.float32), axis=2)
    segment = segment_ids[0]
    seg_branch = segment_branch[0]
    token_branch = jnp.sum(
        jnp.where(
            segment[:, None] == jnp.arange(SEGS, dtype=jnp.int32)[None, :], seg_branch[None, :], 0
        ),
        axis=1,
    )
    row_index = lax.axis_index("rows")
    lengths = lax.dynamic_slice_in_dim(branch_len, row_index * BR_DEV, BR_DEV, 0)
    run_keys = partial(sweep_keys, query_heads, grad_heads, log_norm, row_delta)

    def every_key(offset, count_rows):
        return jnp.ones((tokens, count_rows), dtype=bool)

    query_part, piece_grads = run_keys(
        lax.all_gather(root_kv, "cols", axis=0, tiled=True), every_key
    )
    root_grads = piece_grads
    query_grad = query_part
    piece = lax.all_gather(branch_kv, "cols", axis=1, tiled=True)
    branch_query_grad = query_grad
    updates = []
    for slot in range(BR_DEV):

        def slot_allowed(offset, count_rows, slot=slot):
            slot_pos = offset + jnp.arange(count_rows, dtype=jnp.int32)
            return (token_branch == slot)[:, None] & (slot_pos < lengths[slot])[None, :]

        query_part, piece_grads = run_keys(piece[slot], slot_allowed)
        branch_query_grad = branch_query_grad + query_part
        updates.append(piece_grads)
    branch_grads = jnp.stack(updates)
    query_grad = branch_query_grad
    positions = jnp.arange(tokens, dtype=jnp.int32)

    def leaf_allowed(offset, count_rows):
        key_pos = offset + jnp.arange(count_rows, dtype=jnp.int32)
        return (segment[:, None] == segment[None, :]) & (key_pos[None, :] <= positions[:, None])

    leaf_part, leaf_grads = run_keys(leaf_kv, leaf_allowed)
    query_grad = query_grad + leaf_part
    branch_grad = lax.psum_scatter(branch_grads, "cols", scatter_dimension=1, tiled=True)
    row_whole = lax.psum(root_grads, "rows")
    root_grad = lax.psum_scatter(row_whole, "cols", scatter_dimension=0, tiled=True)
    return (
        query_grad.reshape(tokens, HEADS * HD).astype(jnp.bfloat16),
        leaf_grads,
        root_grad,
        branch_grad,
    )


def solution(mesh):
    in_specs = (
        P(("rows", "cols"), None),
        P(("rows", "cols"), None),
        P(("rows", "cols"), None),
        P(("rows", "cols"), None),
        P(("rows", "cols"), None),
        P("cols", None),
        P("rows", "cols", None),
        P(),
        P(("rows", "cols"), None),
        P(("rows", "cols"), None),
    )
    out_specs = (
        P(("rows", "cols"), None),
        P(("rows", "cols"), None),
        P("cols", None),
        P("rows", "cols", None),
    )
    return jax.shard_map(shards, mesh=mesh, in_specs=in_specs, out_specs=out_specs, check_vma=False)
```

profile of v0, /device:TPU:0, one launch (start us, length us, event | category | flops | bytes accessed | tf_op | source)
XLA Modules:
  0.0 288.9 jit_solution(9851445871758798752)
XLA Ops:
  8.8 1.2 copy.59
  10.0 1.2 copy.58
  11.3 1.2 copy.60
  14.1 36.6 %all-gather.5.cloned.1.call-done = bf16[2,1024,256]{2,1,0:T(8,128)(2,1)} async-done(((bf16[2,64,256]{2,1,0:T(8,128)(2,1)}), bf16[2,1024,256]{2,1,0:T(8,128)(2,1)}) %all-gather.5.cloned.1.call-update) | async-done | bytes 1048592 | tf_op jit(solution)/shard_map/all_gather | solution.py:92
  50.8 2.2 slice_bitcast_fusion.1
  53.0 1.1 broadcast.152.clone2
  54.1 24.9 %while.46 = (s32[]{:T(128)}, f32[256,8,128]{2,0,1:T(8,128)}, f32[2,512,256]{2,1,0:T(8,128)}, s32[256]{0:T(256)S(1)}, s32[2]{0:T(128)S(1)}, /*index=5*/s32[2]{0:T...) while((s32[]{:T(128)}, f32[256,8,128]{2,0,1:T(8,128)}, ...), condition=%wide.region_7.8_spmd.clone, body=%wide.region_6.7_spmd.clone.sunk | while | flops 1353778432 | bytes 27552528 | solution.py:49
  56.8 1.6 fusion.157
  58.4 1.0 fusion.160
  59.4 2.3 fusion.158
  62.5 2.7 fusion.159
  69.0 1.6 fusion.157
  71.6 2.3 fusion.158
  74.7 3.1 %fusion.159 = f32[256,8,128]{2,0,1:T(8,128)} fusion(bf16[256,8,512]{0,2,1:T(8,128)(2,1)S(1)} %fusion.158, f32[256,8,128]{2,0,1:T(8,128)} %get-tuple-element.584, pred[]{:T(512)S(6)} %compare.11, bf16[1024,256]{1,0:T(8,128)(2,1)} %get-tuple-element.605, s32[]{:T(128)S(6)} %select_n.70), kind=kOutput, calls=%fused_computation.54.clone.1 | convolution fusion | flops 269221888 | bytes 4325381 | tf_op jit(solution)/shard_map/while/body/eval_jaxpr/thk,kd->thd/dot_general | solution.py:27
  78.9 10.9 %all-gather.3.cloned.1.call-done = bf16[2048,256]{1,0:T(8,128)(2,1)} async-done(((bf16[128,256]{1,0:T(8,128)(2,1)}), bf16[2048,256]{1,0:T(8,128)(2,1)}) %all-gather.3.cloned.1.call-update) | async-done | bytes 1048592 | tf_op jit(solution)/shard_map/all_gather | solution.py:88
  89.9 42.4 %while.44 = (s32[]{:T(128)}, f32[256,8,128]{2,0,1:T(8,128)}, f32[4,512,256]{2,1,0:T(8,128)}, s32[4]{0:T(128)S(1)}, bf16[2048,256]{1,0:T(8,128)(2,1)}, /*index=5*...) while((s32[]{:T(128)}, f32[256,8,128]{2,0,1:T(8,128)}, ...), condition=%wide.region_2.3_spmd.clone, body=%wide.region_1.2_spmd.clone.sunk | while | flops 1351548928 | bytes 27156720 | solution.py:49
  91.1 1.6 fusion.134
  93.6 2.0 multiply_convert_fusion.3
  96.4 2.6 fusion.135
  101.4 1.6 fusion.134
  103.9 2.0 multiply_convert_fusion.3
  106.7 3.0 %fusion.135 = f32[256,8,128]{2,0,1:T(8,128)} fusion(bf16[512,256,8]{1,0,2:T(8,128)(2,1)S(1)} %multiply_convert_fusion.3, f32[256,8,128]{2,0,1:T(8,128)} %get-tuple-element.630, pred[]{:T(512)S(6)} %compare.9, bf16[2048,256]{1,0:T(8,128)(2,1)} %get-tuple-element.647, s32[]{:T(128)S(6)} %select_n.64), kind=kOutput, calls=%fused_computation.12.clone.1 | convolution fusion | flops 269221888 | bytes 4325381 | tf_op jit(solution)/shard_map/while/body/eval_jaxpr/thk,kd->thd/dot_general | solution.py:27
  112.1 1.6 fusion.134
  114.6 2.0 multiply_convert_fusion.3
  117.4 3.0 %fusion.135 = f32[256,8,128]{2,0,1:T(8,128)} fusion(bf16[512,256,8]{1,0,2:T(8,128)(2,1)S(1)} %multiply_convert_fusion.3, f32[256,8,128]{2,0,1:T(8,128)} %get-tuple-element.630, pred[]{:T(512)S(6)} %compare.9, bf16[2048,256]{1,0:T(8,128)(2,1)} %get-tuple-element.647, s32[]{:T(128)S(6)} %select_n.64), kind=kOutput, calls=%fused_computation.12.clone.1 | convolution fusion | flops 269221888 | bytes 4325381 | tf_op jit(solution)/shard_map/while/body/eval_jaxpr/thk,kd->thd/dot_general | solution.py:27
  122.8 1.6 fusion.134
  125.3 2.0 multiply_convert_fusion.3
  128.1 3.0 %fusion.135 = f32[256,8,128]{2,0,1:T(8,128)} fusion(bf16[512,256,8]{1,0,2:T(8,128)(2,1)S(1)} %multiply_convert_fusion.3, f32[256,8,128]{2,0,1:T(8,128)} %get-tuple-element.630, pred[]{:T(512)S(6)} %compare.9, bf16[2048,256]{1,0:T(8,128)(2,1)} %get-tuple-element.647, s32[]{:T(128)S(6)} %select_n.64), kind=kOutput, calls=%fused_computation.12.clone.1 | convolution fusion | flops 269221888 | bytes 4325381 | tf_op jit(solution)/shard_map/while/body/eval_jaxpr/thk,kd->thd/dot_general | solution.py:27
  132.5 1.1 broadcast.152.clone2.1
  133.6 17.1 %while.45 = (s32[]{:T(128)}, f32[256,8,128]{2,0,1:T(8,128)S(1)}, f32[2,512,256]{2,1,0:T(8,128)}, s32[256]{0:T(256)S(1)}, s32[2]{0:T(128)S(1)}, /*index=5*/s32[2]...) while((s32[]{:T(128)}, f32[256,8,128]{2,0,1:T(8,128)S(1)}, ...), condition=%wide.region_5.6_spmd.clone, body=%wide.region_4.5_spmd.clone.sunk | while | flops 1353778432 | bytes 29649700 | solution.py:49
  135.0 1.6 fusion.145
  136.6 1.0 fusion.148
  137.7 1.4 fusion.146
  139.9 1.1 fusion.147
  143.5 1.6 fusion.145
  145.2 1.0 fusion.148
  146.2 1.4 fusion.146
  148.4 1.1 fusion.147
  150.7 3.0 %pad_maximum_fusion = f32[2,1024,256]{2,1,0:T(8,128)} fusion(f32[1,1024,256]{2,1,0:T(8,128)} %bitcast.248, f32[1,1024,256]{2,1,0:T(8,128)} %bitcast.247), kind=kLoop, calls=%fused_computation.70 | loop fusion | flops 524288 | bytes 4194304 | tf_op jit(solution)/shard_map/stack | solution.py:104
  156.7 1.6 copy.63
  158.3 1.3 copy.62
  159.6 1.6 copy.61
  161.2 32.0 %reduce-scatter.5.cloned.1.call-done = f32[128,256]{1,0:T(8,128)} async-done(((f32[2048,256]{1,0:T(8,128)}), f32[128,256]{1,0:T(8,128)}) %reduce-scatter.5.cloned.1.call-update) | async-done | bytes 131088 | tf_op jit(solution)/shard_map/reduce_scatter | solution.py:116
  193.2 2.5 fusion.60
  195.8 2.0 copy.70
  197.8 60.3 %reduce-scatter.3.cloned.1.call-done = f32[2,64,256]{2,1,0:T(8,128)} async-done(((f32[2,1024,256]{2,1,0:T(8,128)}), f32[2,64,256]{2,1,0:T(8,128)}) %reduce-scatter.3.cloned.1.call-update) | async-done | bytes 131088 | tf_op jit(solution)/shard_map/reduce_scatter | solution.py:114
  258.1 22.6 %all-reduce.2.cloned.1.call-done = f32[128,256]{1,0:T(8,128)} async-done(((f32[128,256]{1,0:T(8,128)}), f32[128,256]{1,0:T(8,128)}) %all-reduce.2.cloned.1.call-update) | async-done | bytes 131088 | tf_op jit(solution)/shard_map/psum | solution.py:115
  280.8 1.6 copy.135
  (96 shorter events, 34.0 us)
Async XLA Ops:
  7.2 43.6 %all-gather.5.cloned.1.call-start = ((), (), s32[]{:S(2)}) async-start(), calls=%async_computation.3 | async-start | bytes 1114112 | tf_op jit(solution)/shard_map/all_gather | solution.py:92
  7.9 82.0 %all-gather.3.cloned.1.call-start = ((), (), s32[]{:S(2)}) async-start(), calls=%async_computation.2 | async-start | bytes 1114112 | tf_op jit(solution)/shard_map/all_gather | solution.py:88
  8.6 184.6 %reduce-scatter.5.cloned.1.call-start = ((), (), s32[]{:S(2)}) async-start(), calls=%async_computation.5 | async-start | bytes 2228224 | tf_op jit(solution)/shard_map/reduce_scatter | solution.py:116
  8.7 45.3 %copy-start.1 = (f32[256,8]{0,1:T(8,128)S(1)}, f32[256,8]{0,1:T(8,128)}, u32[]{:S(2)}) copy-start(f32[256,8]{0,1:T(8,128)} %param.19) | copy-start | bytes 24580
  132.3 125.9 %reduce-scatter.3.cloned.1.call-start = ((), (), s32[]{:S(2)}) async-start(), calls=%async_computation.4 | async-start | bytes 2228224 | tf_op jit(solution)/shard_map/reduce_scatter | solution.py:114
  136.6 1.1 copy-start
  145.1 1.1 copy-start
  150.7 3.1 %copy-start.3 = (s32[1,256]{1,0:T(1,128)S(1)}, s32[1,256]{1,0:T(1,128)}, u32[]{:S(2)}) copy-start(s32[1,256]{1,0:T(1,128)} %param.24) | copy-start | bytes 3076
  150.7 3.2 %copy-start.2 = (bf16[256,256]{1,0:T(8,128)(2,1)S(1)}, bf16[256,256]{1,0:T(8,128)(2,1)}, u32[]{:S(2)}) copy-start(bf16[256,256]{1,0:T(8,128)(2,1)} %param.20) | copy-start | bytes 393220
  153.7 127.0 %all-reduce.2.cloned.1.call-start = ((), (), s32[]{:S(2)}) async-start(), calls=%async_computation.6 | async-start | bytes 262144 | tf_op jit(solution)/shard_map/psum | solution.py:115
Sparse Core Ops, SparseCore 0:
  10.2 40.5 all-gather.4
  52.9 36.8 all-gather.2
  132.4 60.7 reduce-scatter.4
  197.4 60.7 reduce-scatter.2
  260.3 20.4 all-reduce.1
where the time goes:
time: 290 us; the launch traced here: 289 us
  waiting for transfers between devices  164 us (57%)
  matrix products  66.6 us (23%)
  local copies, waits for them, and re-layouts  32.1 us (11%)
  between operations  13.9 us (5%)
  other arithmetic  6.25 us (2%)
  loops' own time  5.64 us (2%)
    reduce_scatter x1, waiting for transfers between devices, shards(): lax.psum_scatter(branch_grads, 'cols', scatter_dimension=1, tiled=True)  60.3 us
    all_gather x1, waiting for transfers between devices, shards(): piece = lax.all_gather(branch_kv, 'cols', axis=1, tiled=True)  36.6 us
    reduce_scatter x1, waiting for transfers between devices, shards(): lax.psum_scatter(row_whole, 'cols', scatter_dimension=0, tiled=True)  32 us
    psum x1, waiting for transfers between devices, shards(): row_whole = lax.psum(root_grads, 'rows')  22.6 us
    dot_general x9, matrix products, block_grads(): jnp.einsum('thk,kd->thd', dscore_b, keys_part, preferred_element_type=jnp...  22.4 us
    dot_general x9, matrix products, block_grads(): jnp.einsum('thd,kd->thk', grad_heads, values_part, preferred_element_type...  15.8 us
    dot_general x9, matrix products, block_grads(): jnp.einsum('thd,kd->thk', query_heads, keys_part, preferred_element_type=...  13.5 us
    all_gather x1, waiting for transfers between devices, shards(): lax.all_gather(root_kv, 'cols', axis=0, tiled=True)  10.9 us
  transfers between devices with their start and end apart: 5, of which 5 were waited for; matrix products, arithmetic and copies ran while one was open for 22% of the time, Pallas kernels for 0%

commit v1 on v0

--- a/solution.py
+++ b/solution.py
@@ -89,7 +89,37 @@
     )
     root_grads = piece_grads
     query_grad = query_part
-    piece = lax.all_gather(branch_kv, "cols", axis=1, tiled=True)
+
+    def leaves_measure(t0, pos_dim):
+        peer_axis = "cols"
+        g_now = lax.axis_size(peer_axis)
+        e_next = lax.axis_index(peer_axis)
+        heard, tall, val2 = (g_now, e_next, t0.shape[pos_dim])
+        crops = tuple((u * heard if pp == pos_dim else u for pp, u in enumerate(t0.shape)))
+        base_arr = jnp.zeros(crops, t0.dtype)
+        fresh = lax.dynamic_update_slice_in_dim(base_arr, t0, tall * val2, axis=pos_dim)
+        piece_next = v_now = t0
+        for nth in tuple(range(1, heard // 2 + 1)):
+            piece_next = lax.ppermute(
+                piece_next,
+                axis_name=peer_axis,
+                perm=tuple(((pp, (pp + 1) % heard) for pp in range(heard))),
+            )
+            fresh = lax.dynamic_update_slice_in_dim(
+                fresh, piece_next, (tall - nth) % heard * val2, axis=pos_dim
+            )
+            if 2 * nth < heard:
+                v_now = lax.ppermute(
+                    v_now,
+                    axis_name=peer_axis,
+                    perm=tuple(((pp, (pp - 1) % heard) for pp in range(heard))),
+                )
+                fresh = lax.dynamic_update_slice_in_dim(
+                    fresh, v_now, (tall + nth) % heard * val2, axis=pos_dim
+                )
+        return fresh
+
+    piece = leaves_measure(branch_kv, 1)
     branch_query_grad = query_grad
     updates = []
     for slot in range(BR_DEV):

time: 290 us -> 294 us (1.014)
  starting transfers between devices: 0.38 us -> 33.2 us
  waiting for transfers between devices: 164 us -> 137 us
    all_gather x1 -> x0, waiting for transfers between devices: 36.6 us -> none  [shards(): piece = lax.all_gather(branch_kv, 'cols', axis=1, tiled=True)]
    ppermute x0 -> x15, starting transfers between devices: none -> 32.9 us  [the longest x7 32.9 us: leaves_measure(): lax.ppermute(v_now, axis_name=peer_axis, perm=tuple(((pp, (pp - 1) % hear...]
    ppermute x0 -> x15, waiting for transfers between devices: none -> 23.2 us  [the longest x8 16.2 us: leaves_measure(): lax.ppermute(piece_next, axis_name=peer_axis, perm=tuple(((pp, (pp + 1) %...]
    all_gather x1, waiting for transfers between devices: 10.9 us -> 0.01 us  [shards(): lax.all_gather(root_kv, 'cols', axis=0, tiled=True)]
    unnamed x11 -> x17, local copies, waits for them, and re-layouts: 6.95 us -> 6.96 us
  transfers between devices with their start and end apart: 5 -> 19, of which waited for: 5 -> 15; matrix products, arithmetic and copies ran while one was open for 22% -> 21% of each run, Pallas kernels for 0% -> 0%
where the time goes in v1:
time: 294 us; the launch traced here: 293 us
  waiting for transfers between devices  137 us (47%)
  matrix products  66.6 us (23%)
  starting transfers between devices  33.2 us (11%)
  local copies, waits for them, and re-layouts  30.5 us (10%)
  between operations  14.5 us (5%)
  loops' own time  5.65 us (2%)
  other arithmetic  5.54 us (2%)
    reduce_scatter x1, waiting for transfers between devices, shards(): lax.psum_scatter(branch_grads, 'cols', scatter_dimension=1, tiled=True)  60.5 us
    ppermute x7, starting transfers between devices, leaves_measure(): lax.ppermute(v_now, axis_name=peer_axis, perm=tuple(((pp, (pp - 1) % hear...  32.9 us
    reduce_scatter x1, waiting for transfers between devices, shards(): lax.psum_scatter(row_whole, 'cols', scatter_dimension=0, tiled=True)  30.2 us
    psum x1, waiting for transfers between devices, shards(): row_whole = lax.psum(root_grads, 'rows')  22.6 us
    dot_general x9, matrix products, block_grads(): jnp.einsum('thk,kd->thd', dscore_b, keys_part, preferred_element_type=jnp...  22.3 us
    ppermute x8, waiting for transfers between devices, leaves_measure(): lax.ppermute(piece_next, axis_name=peer_axis, perm=tuple(((pp, (pp + 1) %...  16.2 us
    dot_general x9, matrix products, block_grads(): jnp.einsum('thd,kd->thk', grad_heads, values_part, preferred_element_type...  15.8 us
    dot_general x9, matrix products, block_grads(): jnp.einsum('thd,kd->thk', query_heads, keys_part, preferred_element_type=...  13.5 us
  transfers between devices with their start and end apart: 19, of which 15 were waited for; matrix products, arithmetic and copies ran while one was open for 21% of the time, Pallas kernels for 0%

profile of v1, /device:TPU:0, one launch (start us, length us, event | category | flops | bytes accessed | tf_op | source)
XLA Modules:
  0.0 292.5 jit_solution(3403272012570976592)
XLA Ops:
  7.3 5.5 %collective-permute-start.1 = (bf16[2,64,256]{2,1,0:T(8,128)(2,1)}, bf16[2,64,256]{2,1,0:T(8,128)(2,1)S(1)}, u32[]{:S(2)}, u32[]{:S(2)}) collective-permute-start(bf16[2,64,256]{2,1,0:T(8,128)(2,1)} %param.22), channel_id=1, source_target_pairs={{0,15},{1,0},{2,1},{3,2},{4,3},{5,4},{6,5},{7,6},{8,7},{9,8},{10,9... | collective-permute-start | bytes 196616 | tf_op jit(solution)/shard_map/ppermute | solution.py:112
  15.7 1.2 copy.60
  17.5 4.5 %collective-permute-start.3 = (bf16[2,64,256]{2,1,0:T(8,128)(2,1)S(1)}, bf16[2,64,256]{2,1,0:T(8,128)(2,1)S(1)}, u32[]{:S(2)}, u32[]{:S(2)}) collective-permute-start(bf16[2,64,256]{2,1,0:T(8,128)(2,1)S(1)} %collective-permute-done.1), channel_id=1, source_target_pairs={{0,15},{1,0},{2,1},{3,2},{4,3},{5,4},{6,5},{7,6},{8,7},{9,8},{10,9... | collective-permute-start | bytes 196616 | tf_op jit(solution)/shard_map/ppermute | solution.py:112
  22.0 2.1 collective-permute-done.3
  24.0 4.6 %collective-permute-start.5 = (bf16[2,64,256]{2,1,0:T(8,128)(2,1)S(1)}, bf16[2,64,256]{2,1,0:T(8,128)(2,1)S(1)}, u32[]{:S(2)}, u32[]{:S(2)}) collective-permute-start(bf16[2,64,256]{2,1,0:T(8,128)(2,1)S(1)} %collective-permute-done.3), channel_id=1, source_target_pairs={{0,15},{1,0},{2,1},{3,2},{4,3},{5,4},{6,5},{7,6},{8,7},{9,8},{10,9... | collective-permute-start | bytes 196616 | tf_op jit(solution)/shard_map/ppermute | solution.py:112
  29.0 1.5 collective-permute-done.5
  30.5 4.6 %collective-permute-start.7 = (bf16[2,64,256]{2,1,0:T(8,128)(2,1)S(1)}, bf16[2,64,256]{2,1,0:T(8,128)(2,1)S(1)}, u32[]{:S(2)}, u32[]{:S(2)}) collective-permute-start(bf16[2,64,256]{2,1,0:T(8,128)(2,1)S(1)} %collective-permute-done.5), channel_id=1, source_target_pairs={{0,15},{1,0},{2,1},{3,2},{4,3},{5,4},{6,5},{7,6},{8,7},{9,8},{10,9... | collective-permute-start | bytes 196616 | tf_op jit(solution)/shard_map/ppermute | solution.py:112
  35.8 1.3 collective-permute-done.7
  37.1 4.5 %collective-permute-start.9 = (bf16[2,64,256]{2,1,0:T(8,128)(2,1)S(1)}, bf16[2,64,256]{2,1,0:T(8,128)(2,1)S(1)}, u32[]{:S(2)}, u32[]{:S(2)}) collective-permute-start(bf16[2,64,256]{2,1,0:T(8,128)(2,1)S(1)} %collective-permute-done.7), channel_id=1, source_target_pairs={{0,15},{1,0},{2,1},{3,2},{4,3},{5,4},{6,5},{7,6},{8,7},{9,8},{10,9... | collective-permute-start | bytes 196616 | tf_op jit(solution)/shard_map/ppermute | solution.py:112
  43.5 4.6 %collective-permute-start.11 = (bf16[2,64,256]{2,1,0:T(8,128)(2,1)S(1)}, bf16[2,64,256]{2,1,0:T(8,128)(2,1)S(1)}, u32[]{:S(2)}, u32[]{:S(2)}) collective-permute-start(bf16[2,64,256]{2,1,0:T(8,128)(2,1)S(1)} %collective-permute-done.9), channel_id=1, source_target_pairs={{0,15},{1,0},{2,1},{3,2},{4,3},{5,4},{6,5},{7,6},{8,7},{9,8},{10,9... | collective-permute-start | bytes 196616 | tf_op jit(solution)/shard_map/ppermute | solution.py:112
  50.0 4.6 %collective-permute-start.13 = (bf16[2,64,256]{2,1,0:T(8,128)(2,1)S(1)}, bf16[2,64,256]{2,1,0:T(8,128)(2,1)S(1)}, u32[]{:S(2)}, u32[]{:S(2)}) collective-permute-start(bf16[2,64,256]{2,1,0:T(8,128)(2,1)S(1)} %collective-permute-done.11), channel_id=1, source_target_pairs={{0,15},{1,0},{2,1},{3,2},{4,3},{5,4},{6,5},{7,6},{8,7},{9,8},{10,9... | collective-permute-start | bytes 196616 | tf_op jit(solution)/shard_map/ppermute | solution.py:112
  55.5 6.4 %collective-permute-done.12 = bf16[2,64,256]{2,1,0:T(8,128)(2,1)S(1)} collective-permute-done((bf16[2,64,256]{2,1,0:T(8,128)(2,1)S(1)}, bf16[2,64,256]{2,1,0:T(8,128)(2,1)S(1)}, u32[]{:S(2)}, u32[]{:S(2)}) %collective-permute-start.12) | collective-permute-done | bytes 65568 | tf_op jit(solution)/shard_map/ppermute | solution.py:103
  61.9 6.3 %collective-permute-done.14 = bf16[2,64,256]{2,1,0:T(8,128)(2,1)S(1)} collective-permute-done((bf16[2,64,256]{2,1,0:T(8,128)(2,1)S(1)}, bf16[2,64,256]{2,1,0:T(8,128)(2,1)S(1)}, u32[]{:S(2)}, u32[]{:S(2)}) %collective-permute-start.14) | collective-permute-done | bytes 65568 | tf_op jit(solution)/shard_map/ppermute | solution.py:103
  70.3 24.8 %while.46 = (s32[]{:T(128)}, f32[256,8,128]{2,0,1:T(8,128)}, f32[2,512,256]{2,1,0:T(8,128)}, s32[256]{0:T(256)S(1)}, s32[2]{0:T(128)S(1)}, /*index=5*/s32[2]{0:T...) while((s32[]{:T(128)}, f32[256,8,128]{2,0,1:T(8,128)}, ...), condition=%wide.region_7.8_spmd.clone, body=%wide.region_6.7_spmd.clone.sunk | while | flops 1353778432 | bytes 27552528 | solution.py:49
  73.0 1.6 fusion.157
  75.7 2.3 fusion.158
  78.8 2.7 fusion.159
  85.2 1.6 fusion.157
  87.9 2.3 fusion.158
  91.0 3.1 %fusion.159 = f32[256,8,128]{2,0,1:T(8,128)} fusion(bf16[256,8,512]{0,2,1:T(8,128)(2,1)S(1)} %fusion.158, f32[256,8,128]{2,0,1:T(8,128)} %get-tuple-element.584, pred[]{:T(512)S(6)} %compare.26, bf16[1024,256]{1,0:T(8,128)(2,1)} %get-tuple-element.605, s32[]{:T(128)S(6)} %select_n.212), kind=kOutput, calls=%fused_computation.54.clone.1 | convolution fusion | flops 269221888 | bytes 4325381 | tf_op jit(solution)/shard_map/while/body/eval_jaxpr/thk,kd->thd/dot_general | solution.py:27
  95.1 42.5 %while.44 = (s32[]{:T(128)}, f32[256,8,128]{2,0,1:T(8,128)}, f32[4,512,256]{2,1,0:T(8,128)}, s32[4]{0:T(128)S(1)}, bf16[2048,256]{1,0:T(8,128)(2,1)}, /*index=5*...) while((s32[]{:T(128)}, f32[256,8,128]{2,0,1:T(8,128)}, ...), condition=%wide.region_2.3_spmd.clone, body=%wide.region_1.2_spmd.clone.sunk | while | flops 1351548928 | bytes 27156720 | solution.py:49
  96.3 1.6 fusion.134
  98.9 2.0 multiply_convert_fusion.3
  101.7 2.7 fusion.135
  106.7 1.6 fusion.134
  109.2 2.0 multiply_convert_fusion.3
  112.0 3.1 %fusion.135 = f32[256,8,128]{2,0,1:T(8,128)} fusion(bf16[512,256,8]{1,0,2:T(8,128)(2,1)S(1)} %multiply_convert_fusion.3, f32[256,8,128]{2,0,1:T(8,128)} %get-tuple-element.630, pred[]{:T(512)S(6)} %compare.24, bf16[2048,256]{1,0:T(8,128)(2,1)} %get-tuple-element.647, s32[]{:T(128)S(6)} %select_n.206), kind=kOutput, calls=%fused_computation.12.clone.1 | convolution fusion | flops 269221888 | bytes 4325381 | tf_op jit(solution)/shard_map/while/body/eval_jaxpr/thk,kd->thd/dot_general | solution.py:27
  117.4 1.6 fusion.134
  119.9 2.0 multiply_convert_fusion.3
  122.7 3.1 %fusion.135 = f32[256,8,128]{2,0,1:T(8,128)} fusion(bf16[512,256,8]{1,0,2:T(8,128)(2,1)S(1)} %multiply_convert_fusion.3, f32[256,8,128]{2,0,1:T(8,128)} %get-tuple-element.630, pred[]{:T(512)S(6)} %compare.24, bf16[2048,256]{1,0:T(8,128)(2,1)} %get-tuple-element.647, s32[]{:T(128)S(6)} %select_n.206), kind=kOutput, calls=%fused_computation.12.clone.1 | convolution fusion | flops 269221888 | bytes 4325381 | tf_op jit(solution)/shard_map/while/body/eval_jaxpr/thk,kd->thd/dot_general | solution.py:27
  128.1 1.6 fusion.134
  130.6 2.0 multiply_convert_fusion.3
  133.4 3.1 %fusion.135 = f32[256,8,128]{2,0,1:T(8,128)} fusion(bf16[512,256,8]{1,0,2:T(8,128)(2,1)S(1)} %multiply_convert_fusion.3, f32[256,8,128]{2,0,1:T(8,128)} %get-tuple-element.630, pred[]{:T(512)S(6)} %compare.24, bf16[2048,256]{1,0:T(8,128)(2,1)} %get-tuple-element.647, s32[]{:T(128)S(6)} %select_n.206), kind=kOutput, calls=%fused_computation.12.clone.1 | convolution fusion | flops 269221888 | bytes 4325381 | tf_op jit(solution)/shard_map/while/body/eval_jaxpr/thk,kd->thd/dot_general | solution.py:27
  139.0 17.1 %while.45 = (s32[]{:T(128)}, f32[256,8,128]{2,0,1:T(8,128)S(1)}, f32[2,512,256]{2,1,0:T(8,128)}, s32[256]{0:T(256)S(1)}, s32[2]{0:T(128)S(1)}, /*index=5*/s32[2]...) while((s32[]{:T(128)}, f32[256,8,128]{2,0,1:T(8,128)S(1)}, ...), condition=%wide.region_5.6_spmd.clone, body=%wide.region_4.5_spmd.clone.sunk | while | flops 1353778432 | bytes 29649700 | solution.py:49
  140.4 1.6 fusion.145
  143.1 1.4 fusion.146
  148.9 1.6 fusion.145
  151.6 1.4 fusion.146
  156.1 3.0 %pad_maximum_fusion = f32[2,1024,256]{2,1,0:T(8,128)} fusion(f32[1,1024,256]{2,1,0:T(8,128)} %bitcast.248, f32[1,1024,256]{2,1,0:T(8,128)} %bitcast.247), kind=kLoop, calls=%fused_computation.70 | loop fusion | flops 524288 | bytes 4194304 | tf_op jit(solution)/shard_map/stack | solution.py:134
  162.1 1.6 copy.63
  163.7 1.3 copy.62
  165.0 1.6 copy.61
  166.5 30.2 %reduce-scatter.5.cloned.1.call-done = f32[128,256]{1,0:T(8,128)} async-done(((f32[2048,256]{1,0:T(8,128)}), f32[128,256]{1,0:T(8,128)}) %reduce-scatter.5.cloned.1.call-update) | async-done | bytes 131088 | tf_op jit(solution)/shard_map/reduce_scatter | solution.py:146
  196.7 2.5 fusion.60
  199.3 2.0 copy.70
  201.3 60.5 %reduce-scatter.3.cloned.1.call-done = f32[2,64,256]{2,1,0:T(8,128)} async-done(((f32[2,1024,256]{2,1,0:T(8,128)}), f32[2,64,256]{2,1,0:T(8,128)}) %reduce-scatter.3.cloned.1.call-update) | async-done | bytes 131088 | tf_op jit(solution)/shard_map/reduce_scatter | solution.py:144
  261.8 22.6 %all-reduce.2.cloned.1.call-done = f32[128,256]{1,0:T(8,128)} async-done(((f32[128,256]{1,0:T(8,128)}), f32[128,256]{1,0:T(8,128)}) %all-reduce.2.cloned.1.call-update) | async-done | bytes 131088 | tf_op jit(solution)/shard_map/psum | solution.py:145
  284.4 1.6 copy.151
  (146 shorter events, 48.1 us)
Async XLA Ops:
  7.2 10.1 %copy-start.3 = (bf16[2,64,256]{2,1,0:T(8,128)(2,1)S(1)}, bf16[2,64,256]{2,1,0:T(8,128)(2,1)}, u32[]{:S(2)}) copy-start(bf16[2,64,256]{2,1,0:T(8,128)(2,1)} %param.22) | copy-start | bytes 196612
  7.2 9.8 %copy-start.6 = (s32[4]{0:T(128)S(1)}, s32[4]{0:T(128)}, u32[]{:S(2)}) copy-start(s32[4]{0:T(128)} %param.23) | copy-start | bytes 52
  7.2 10.2 %copy-start.5 = (s32[1,8]{1,0:T(1,128)S(1)}, s32[1,8]{1,0:T(1,128)}, u32[]{:S(2)}) copy-start(s32[1,8]{1,0:T(1,128)} %param.25) | copy-start | bytes 100
  7.2 10.2 %copy-start.4 = (s32[1,256]{1,0:T(1,128)S(1)}, s32[1,256]{1,0:T(1,128)}, u32[]{:S(2)}) copy-start(s32[1,256]{1,0:T(1,128)} %param.24) | copy-start | bytes 3076
  7.2 87.9 %all-gather.2.cloned.1.call-start = ((), (), s32[]{:S(2)}) async-start(), calls=%async_computation.2 | async-start | bytes 1114112 | tf_op jit(solution)/shard_map/all_gather | solution.py:88
  7.3 10.2 %collective-permute-start.1 = (bf16[2,64,256]{2,1,0:T(8,128)(2,1)}, bf16[2,64,256]{2,1,0:T(8,128)(2,1)S(1)}, u32[]{:S(2)}, u32[]{:S(2)}) collective-permute-start(bf16[2,64,256]{2,1,0:T(8,128)(2,1)} %param.22), channel_id=1, source_target_pairs={{0,15},{1,0},{2,1},{3,2},{4,3},{5,4},{6,5},{7,6},{8,7},{9,8},{10,9... | collective-permute-start | bytes 196616 | tf_op jit(solution)/shard_map/ppermute | solution.py:112
  12.8 9.2 %collective-permute-start = (bf16[2,64,256]{2,1,0:T(8,128)(2,1)}, bf16[2,64,256]{2,1,0:T(8,128)(2,1)S(1)}, u32[]{:S(2)}, u32[]{:S(2)}) collective-permute-start(bf16[2,64,256]{2,1,0:T(8,128)(2,1)} %param.22), channel_id=1, source_target_pairs={{0,1},{1,2},{2,3},{3,4},{4,5},{5,6},{6,7},{7,8},{8,9},{9,10},{10,1... | collective-permute-start | bytes 196616 | tf_op jit(solution)/shard_map/ppermute | solution.py:103
  12.8 183.9 %reduce-scatter.5.cloned.1.call-start = ((), (), s32[]{:S(2)}) async-start(), calls=%async_computation.4 | async-start | bytes 2228224 | tf_op jit(solution)/shard_map/reduce_scatter | solution.py:146
  16.9 53.4 %copy-start.1 = (f32[256,8]{0,1:T(8,128)S(1)}, f32[256,8]{0,1:T(8,128)}, u32[]{:S(2)}) copy-start(f32[256,8]{0,1:T(8,128)} %param.19) | copy-start | bytes 24580
  17.5 6.6 %collective-permute-start.3 = (bf16[2,64,256]{2,1,0:T(8,128)(2,1)S(1)}, bf16[2,64,256]{2,1,0:T(8,128)(2,1)S(1)}, u32[]{:S(2)}, u32[]{:S(2)}) collective-permute-start(bf16[2,64,256]{2,1,0:T(8,128)(2,1)S(1)} %collective-permute-done.1), channel_id=1, source_target_pairs={{0,15},{1,0},{2,1},{3,2},{4,3},{5,4},{6,5},{7,6},{8,7},{9,8},{10,9... | collective-permute-start | bytes 196616 | tf_op jit(solution)/shard_map/ppermute | solution.py:112
  21.9 7.0 %collective-permute-start.2 = (bf16[2,64,256]{2,1,0:T(8,128)(2,1)S(1)}, bf16[2,64,256]{2,1,0:T(8,128)(2,1)S(1)}, u32[]{:S(2)}, u32[]{:S(2)}) collective-permute-start(bf16[2,64,256]{2,1,0:T(8,128)(2,1)S(1)} %collective-permute-done), channel_id=1, source_target_pairs={{0,1},{1,2},{2,3},{3,4},{4,5},{5,6},{6,7},{7,8},{8,9},{9,10},{10,1... | collective-permute-start | bytes 196616 | tf_op jit(solution)/shard_map/ppermute | solution.py:103
  24.0 6.5 %collective-permute-start.5 = (bf16[2,64,256]{2,1,0:T(8,128)(2,1)S(1)}, bf16[2,64,256]{2,1,0:T(8,128)(2,1)S(1)}, u32[]{:S(2)}, u32[]{:S(2)}) collective-permute-start(bf16[2,64,256]{2,1,0:T(8,128)(2,1)S(1)} %collective-permute-done.3), channel_id=1, source_target_pairs={{0,15},{1,0},{2,1},{3,2},{4,3},{5,4},{6,5},{7,6},{8,7},{9,8},{10,9... | collective-permute-start | bytes 196616 | tf_op jit(solution)/shard_map/ppermute | solution.py:112
  29.0 6.8 %collective-permute-start.4 = (bf16[2,64,256]{2,1,0:T(8,128)(2,1)S(1)}, bf16[2,64,256]{2,1,0:T(8,128)(2,1)S(1)}, u32[]{:S(2)}, u32[]{:S(2)}) collective-permute-start(bf16[2,64,256]{2,1,0:T(8,128)(2,1)S(1)} %collective-permute-done.2), channel_id=1, source_target_pairs={{0,1},{1,2},{2,3},{3,4},{4,5},{5,6},{6,7},{7,8},{8,9},{9,10},{10,1... | collective-permute-start | bytes 196616 | tf_op jit(solution)/shard_map/ppermute | solution.py:103
  30.5 6.5 %collective-permute-start.7 = (bf16[2,64,256]{2,1,0:T(8,128)(2,1)S(1)}, bf16[2,64,256]{2,1,0:T(8,128)(2,1)S(1)}, u32[]{:S(2)}, u32[]{:S(2)}) collective-permute-start(bf16[2,64,256]{2,1,0:T(8,128)(2,1)S(1)} %collective-permute-done.5), channel_id=1, source_target_pairs={{0,15},{1,0},{2,1},{3,2},{4,3},{5,4},{6,5},{7,6},{8,7},{9,8},{10,9... | collective-permute-start | bytes 196616 | tf_op jit(solution)/shard_map/ppermute | solution.py:112
  35.7 6.5 %collective-permute-start.6 = (bf16[2,64,256]{2,1,0:T(8,128)(2,1)S(1)}, bf16[2,64,256]{2,1,0:T(8,128)(2,1)S(1)}, u32[]{:S(2)}, u32[]{:S(2)}) collective-permute-start(bf16[2,64,256]{2,1,0:T(8,128)(2,1)S(1)} %collective-permute-done.4), channel_id=1, source_target_pairs={{0,1},{1,2},{2,3},{3,4},{4,5},{5,6},{6,7},{7,8},{8,9},{9,10},{10,1... | collective-permute-start | bytes 196616 | tf_op jit(solution)/shard_map/ppermute | solution.py:103
  37.1 6.4 %collective-permute-start.9 = (bf16[2,64,256]{2,1,0:T(8,128)(2,1)S(1)}, bf16[2,64,256]{2,1,0:T(8,128)(2,1)S(1)}, u32[]{:S(2)}, u32[]{:S(2)}) collective-permute-start(bf16[2,64,256]{2,1,0:T(8,128)(2,1)S(1)} %collective-permute-done.7), channel_id=1, source_target_pairs={{0,15},{1,0},{2,1},{3,2},{4,3},{5,4},{6,5},{7,6},{8,7},{9,8},{10,9... | collective-permute-start | bytes 196616 | tf_op jit(solution)/shard_map/ppermute | solution.py:112
  42.2 6.9 %collective-permute-start.8 = (bf16[2,64,256]{2,1,0:T(8,128)(2,1)S(1)}, bf16[2,64,256]{2,1,0:T(8,128)(2,1)S(1)}, u32[]{:S(2)}, u32[]{:S(2)}) collective-permute-start(bf16[2,64,256]{2,1,0:T(8,128)(2,1)S(1)} %collective-permute-done.6), channel_id=1, source_target_pairs={{0,1},{1,2},{2,3},{3,4},{4,5},{5,6},{6,7},{7,8},{8,9},{9,10},{10,1... | collective-permute-start | bytes 196616 | tf_op jit(solution)/shard_map/ppermute | solution.py:103
  43.5 6.5 %collective-permute-start.11 = (bf16[2,64,256]{2,1,0:T(8,128)(2,1)S(1)}, bf16[2,64,256]{2,1,0:T(8,128)(2,1)S(1)}, u32[]{:S(2)}, u32[]{:S(2)}) collective-permute-start(bf16[2,64,256]{2,1,0:T(8,128)(2,1)S(1)} %collective-permute-done.9), channel_id=1, source_target_pairs={{0,15},{1,0},{2,1},{3,2},{4,3},{5,4},{6,5},{7,6},{8,7},{9,8},{10,9... | collective-permute-start | bytes 196616 | tf_op jit(solution)/shard_map/ppermute | solution.py:112
  49.1 6.4 %collective-permute-start.10 = (bf16[2,64,256]{2,1,0:T(8,128)(2,1)S(1)}, bf16[2,64,256]{2,1,0:T(8,128)(2,1)S(1)}, u32[]{:S(2)}, u32[]{:S(2)}) collective-permute-start(bf16[2,64,256]{2,1,0:T(8,128)(2,1)S(1)} %collective-permute-done.8), channel_id=1, source_target_pairs={{0,1},{1,2},{2,3},{3,4},{4,5},{5,6},{6,7},{7,8},{8,9},{9,10},{10,1... | collective-permute-start | bytes 196616 | tf_op jit(solution)/shard_map/ppermute | solution.py:103
  50.0 11.9 %collective-permute-start.13 = (bf16[2,64,256]{2,1,0:T(8,128)(2,1)S(1)}, bf16[2,64,256]{2,1,0:T(8,128)(2,1)S(1)}, u32[]{:S(2)}, u32[]{:S(2)}) collective-permute-start(bf16[2,64,256]{2,1,0:T(8,128)(2,1)S(1)} %collective-permute-done.11), channel_id=1, source_target_pairs={{0,15},{1,0},{2,1},{3,2},{4,3},{5,4},{6,5},{7,6},{8,7},{9,8},{10,9... | collective-permute-start | bytes 196616 | tf_op jit(solution)/shard_map/ppermute | solution.py:112
  55.5 6.4 %collective-permute-start.12 = (bf16[2,64,256]{2,1,0:T(8,128)(2,1)S(1)}, bf16[2,64,256]{2,1,0:T(8,128)(2,1)S(1)}, u32[]{:S(2)}, u32[]{:S(2)}) collective-permute-start(bf16[2,64,256]{2,1,0:T(8,128)(2,1)S(1)} %collective-permute-done.10), channel_id=1, source_target_pairs={{0,1},{1,2},{2,3},{3,4},{4,5},{5,6},{6,7},{7,8},{8,9},{9,10},{10,1... | collective-permute-start | bytes 196616 | tf_op jit(solution)/shard_map/ppermute | solution.py:103
  61.9 6.4 %collective-permute-start.14 = (bf16[2,64,256]{2,1,0:T(8,128)(2,1)S(1)}, bf16[2,64,256]{2,1,0:T(8,128)(2,1)S(1)}, u32[]{:S(2)}, u32[]{:S(2)}) collective-permute-start(bf16[2,64,256]{2,1,0:T(8,128)(2,1)S(1)} %collective-permute-done.12), channel_id=1, source_target_pairs={{0,1},{1,2},{2,3},{3,4},{4,5},{5,6},{6,7},{7,8},{8,9},{9,10},{10,1... | collective-permute-start | bytes 196616 | tf_op jit(solution)/shard_map/ppermute | solution.py:103
  137.6 124.2 %reduce-scatter.3.cloned.1.call-start = ((), (), s32[]{:S(2)}) async-start(), calls=%async_computation.3 | async-start | bytes 2228224 | tf_op jit(solution)/shard_map/reduce_scatter | solution.py:144
  142.0 1.1 copy-start
  150.5 1.1 copy-start
  156.1 3.2 %copy-start.2 = (bf16[256,256]{1,0:T(8,128)(2,1)S(1)}, bf16[256,256]{1,0:T(8,128)(2,1)}, u32[]{:S(2)}) copy-start(bf16[256,256]{1,0:T(8,128)(2,1)} %param.20) | copy-start | bytes 393220
  159.1 125.3 %all-reduce.2.cloned.1.call-start = ((), (), s32[]{:S(2)}) async-start(), calls=%async_computation.5 | async-start | bytes 262144 | tf_op jit(solution)/shard_map/psum | solution.py:145
Sparse Core Ops, SparseCore 0:
  12.9 40.7 all-gather.1
  137.7 58.9 reduce-scatter.4
  201.0 60.7 reduce-scatter.2
  263.9 20.4 all-reduce.1
